TPU v7x, 32 devices: a whole 2x2x4 slice. The times are simulated.
32 devices in a mesh: tm: 4 (over y, x), aux: 4 (over z), pair: 2 (over core).
Axes of the slice: x: 2, y: 2, z: 4, core: 2. Of those that a mesh axis runs over, the one named last changes fastest.
Arguments:
- factors: bfloat16 [3072, 5120], P('aux', 'pair'), may hold values from -0.078125 to 0.078125
- panel_factors: bfloat16 [256, 5120], P('aux', 'pair'), may hold values from -6 to 6
- time_weights: float32 [12, 5120], P('tm', 'pair'), may hold values from 0.2 to 2
- tile_mask: int32 [24, 40], P('aux', 'pair'), may hold values 0 or 1
- forward_table: float32 [12, 12], replicated, may hold values from -0.5 to 0.5
- screening: float32 [12, 256, 256], P('tm', 'aux'), may hold values from -0.375 to 0.375
- back_table: float32 [12, 12], replicated, may hold values from -0.5 to 0.5
Outputs:
- sigma: float32 [12, 5120], P('tm', 'pair')
All inputs are finite; a program needn't handle non-finite values. No bound on the sum of `tile_mask` on one device may be relied on, other than what follows from the above.
Results may differ from a plain program's by a relative error of at most 0.0003.
Values may be sent and summed in bfloat16 or wider, within the bound.
No kernel may reach another device: no remote copies, remote signals or barrier semaphores. Data moves between devices by JAX's collectives and lax.ppermute only.
A program may use at most 64 MiB of HBM per device.

v0:
```python
import jax
import jax.numpy as jnp
from jax import lax
from jax.sharding import PartitionSpec as P

TILE = 128


def expand_tiles(tile_mask):
    tile_rows, tile_cols = tile_mask.shape
    spread = jnp.broadcast_to(tile_mask[:, None, :, None], (tile_rows, TILE, tile_cols, TILE))
    return spread.reshape(tile_rows * TILE, tile_cols * TILE)


def body(factors, panel_factors, time_weights, tile_mask, forward_table, screening, back_table):
    highest = lax.Precision.HIGHEST
    masked = factors.astype(jnp.float32) * expand_tiles(tile_mask).astype(jnp.float32)
    panel_full = lax.all_gather(panel_factors, "aux", axis=0, tiled=True)
    panel_wide = panel_full.astype(jnp.float32)
    freq_count = screening.shape[0]
    first_freq = lax.axis_index("tm") * freq_count
    weights_all = lax.all_gather(time_weights, "tm", axis=0, tiled=True)
    table_rows = lax.dynamic_slice_in_dim(forward_table, first_freq, freq_count, 0)
    line_weights = jnp.dot(table_rows, weights_all, precision=highest)
    scaled = panel_wide[None, :, :] * line_weights[:, None, :]
    polar_line = jnp.einsum("tpk,qk->tpq", scaled, masked, precision=highest)
    polar_half = lax.psum_scatter(polar_line, "pair", scatter_dimension=2, tiled=True)
    inverse = lax.all_gather(screening, "aux", axis=1, tiled=True)
    screened = jnp.einsum("wpr,wrq->wpq", inverse, polar_half, precision=highest)
    back_cols = lax.dynamic_slice_in_dim(back_table, first_freq, freq_count, 1)
    lines_full = lax.all_gather(screened, "pair", axis=2, tiled=True)
    contracted = jnp.einsum("tpq,qk->tpk", lines_full, masked, precision=highest)
    partial_value = jnp.sum(panel_wide[None, :, :] * contracted, axis=1) * panel_full.shape[0] ** (
        -0.5
    )
    timed = jnp.dot(back_cols, partial_value, precision=highest)
    partial_value = lax.psum_scatter(timed, "tm", scatter_dimension=0, tiled=True)
    return lax.psum(partial_value, "aux")


def solution(mesh):
    placed = (
        P("aux", "pair"),
        P("aux", "pair"),
        P("tm", "pair"),
        P("aux", "pair"),
        P(),
        P("tm", "aux", None),
        P(),
    )
    return jax.shard_map(
        body, mesh=mesh, in_specs=placed, out_specs=P("tm", "pair"), check_vma=False
    )
```

profile of v0, /device:TPU:0, one launch (start us, length us, event | category | flops | bytes accessed | tf_op | source)
XLA Modules:
  0.0 203.3 jit_solution(14828435998711935432)
XLA Ops:
  6.5 0.0 copy-start
  6.5 0.0 all-gather.4.cloned.1.call-start
  6.5 0.7 all-gather.4.cloned.1.call-update
  7.3 0.0 reduce-scatter.2.cloned.1.call-start
  7.3 10.3 %all-gather = f32[4,3,2560]{2,1,0:T(4,128)S(1)} all-gather(f32[1,3,2560]{2,1,0:T(4,128)} %bitcast.22), channel_id=1, replica_groups=mesh['tm'=4,'aux'=4,'pair'=2] {'tm'}, dimensions={0}, use_global_device_ids=true | all-gather | bytes 153600 | tf_op jit(solution)/shard_map/all_gather | solution.py:22
  17.6 0.1 reshape.6
  17.7 0.7 convert_element_type.15
  18.4 0.9 fusion.11
  19.3 24.9 %all-gather.4.cloned.1.call-done = bf16[256,2560]{1,0:T(8,128)(2,1)} async-done(((bf16[64,2560]{1,0:T(8,128)(2,1)}), bf16[256,2560]{1,0:T(8,128)(2,1)}) %all-gather.4.cloned.1.call-update) | async-done | bytes 1310736 | tf_op jit(solution)/shard_map/all_gather | solution.py:18
  44.2 1.6 convert_element_type.13
  45.8 0.0 copy-start.2
  45.8 0.7 broadcast_in_dim.2
  46.5 0.0 copy-start.1
  46.5 3.7 %copy-done.1 = f32[6,128,20,128]{3,2,1,0:T(8,128)} copy-done((f32[6,128,20,128]{3,2,1,0:T(8,128)}, f32[6,128,20,128]{3,2,1,0:T(8,128)S(1)}, u32[]{:S(2)}) %copy-start.1) | copy-done | bytes 7864344
  50.2 0.0 copy-done.2
  50.2 22.1 %fusion.1 = f32[3,256,768]{2,1,0:T(8,128)} fusion(f32[96,8,20,128]{3,2,1,0:T(8,128)S(1)} %bitcast.20, bf16[768,2560]{1,0:T(8,128)(2,1)S(1)} %copy-done.2, f32[3,2560]{1,0:T(4,128)S(1)} %fusion.11, f32[256,2560]{1,0:T(8,128)S(1)} %convert_element_type.13), kind=kOutput, calls=%fused_computation.3 | convolution fusion | flops 18125291520 | bytes 16807936 | tf_op jit(solution)/shard_map/tpk,qk->tpq/dot_general | solution.py:26
  72.3 0.0 reduce-scatter.2.cloned.1.call-update
  72.3 0.0 all-gather.6.cloned.1.call-start
  72.4 18.2 %all_gather.14 = f32[3,256,256]{2,1,0:T(8,128)S(1)} all-gather(f32[3,64,256]{2,1,0:T(8,128)} %param.12), channel_id=1, replica_groups=mesh['tm'=4,'aux'=4,'pair'=2] {'aux'}, dimensions={1}, use_global_device_ids=true | all-gather | bytes 983040 | tf_op jit(solution)/shard_map/all_gather | solution.py:28
  90.6 4.4 %convolution_bitcast_fusion = f32[3,256,384]{1,2,0:T(8,128)} fusion(f32[3,256,384]{2,1,0:T(8,128)} %reduce-scatter.2.cloned.1.call-done, f32[3,256,256]{2,1,0:T(8,128)S(1)} %all_gather.14), kind=kOutput, calls=%fused_computation.7 | convolution fusion | flops 905969664 | bytes 3145728 | tf_op jit(solution)/shard_map/wpr,wrq->wpq/dot_general | solution.py:29
  94.9 0.0 all-gather.6.cloned.1.call-update
  95.0 0.0 copy-start.3
  95.0 0.0 all-reduce.3.cloned.1.call-start
  95.0 10.5 %all-gather.6.cloned.1.call-done = f32[3,256,768]{1,2,0:T(8,128)} async-done(((f32[3,256,384]{1,2,0:T(8,128)}), f32[3,256,768]{1,2,0:T(8,128)}) %all-gather.6.cloned.1.call-update) | async-done | bytes 2359312 | tf_op jit(solution)/shard_map/all_gather | solution.py:31
  105.5 25.5 %multiply_reduce_fusion = f32[3,2560]{1,0:T(4,128)S(1)} fusion(f32[3,256,768]{1,2,0:T(8,128)} %all-gather.6.cloned.1.call-done, f32[96,8,20,128]{3,2,1,0:T(8,128)} %bitcast.21, bf16[768,2560]{1,0:T(8,128)(2,1)} %param.7, f32[256,2560]{1,0:T(8,128)S(1)} %convert_element_type.13), kind=kOutput, calls=%fused_computation.2 | convolution fusion | flops 18127249408 | bytes 16807936 | tf_op jit(solution)/shard_map/tpq,qk->tpk/dot_general | solution.py:32
  131.1 0.0 copy-done
  131.1 1.0 fusion.7
  132.1 0.0 all-reduce.3.cloned.1.call-update
  132.1 0.6 dynamic-slice
  133.4 42.5 %all-reduce.3.cloned.1.call-done = f32[12,2560]{1,0:T(8,128)} async-done(((f32[12,2560]{1,0:T(8,128)}), f32[12,2560]{1,0:T(8,128)}) %all-reduce.3.cloned.1.call-update) | async-done | bytes 122896
  175.9 0.9 constant_dynamic-slice_fusion
  176.8 20.0 %psum.7 = f32[3,2560]{1,0:T(4,128)} all-reduce(f32[3,2560]{1,0:T(4,128)S(1)} %constant_dynamic-slice_fusion), channel_id=1, replica_groups=mesh['tm'=4,'aux'=4,'pair'=2] {'aux'}, use_global_device_ids=true, to_apply=%region_3.0 | all-reduce | flops 7680 | bytes 61440 | tf_op jit(solution)/shard_map/psum | solution.py:38
  (2 shorter events, 0.0 us)
Async XLA Ops:
  6.5 124.5 %copy-start = (f32[12,12]{1,0:T(8,128)S(1)}, f32[12,12]{1,0:T(8,128)}, u32[]{:S(2)}) copy-start(f32[12,12]{1,0:T(8,128)} %param.13) | copy-start | bytes 1732
  6.5 37.7 %all-gather.4.cloned.1.call-start = ((), (), s32[]{:S(2)}) async-start(), calls=%async_computation.1 | async-start | bytes 1638400 | tf_op jit(solution)/shard_map/all_gather | solution.py:18
  7.3 83.3 %reduce-scatter.2.cloned.1.call-start = ((), (), s32[]{:S(2)}) async-start(), calls=%async_computation.2 | async-start | bytes 3538944 | tf_op jit(solution)/shard_map/reduce_scatter | solution.py:27
  45.8 4.4 %copy-start.2 = (bf16[768,2560]{1,0:T(8,128)(2,1)S(1)}, bf16[768,2560]{1,0:T(8,128)(2,1)}, u32[]{:S(2)}) copy-start(bf16[768,2560]{1,0:T(8,128)(2,1)} %param.7) | copy-start | bytes 11796484
  46.5 3.7 %copy-start.1 = (f32[6,128,20,128]{3,2,1,0:T(8,128)}, f32[6,128,20,128]{3,2,1,0:T(8,128)S(1)}, u32[]{:S(2)}) copy-start(f32[6,128,20,128]{3,2,1,0:T(8,128)S(1)} %broadcast_in_dim.2) | copy-start | bytes 23592964
  72.3 33.2 %all-gather.6.cloned.1.call-start = ((), (), s32[]{:S(2)}) async-start(), calls=%async_computation.3 | async-start | bytes 3538944 | tf_op jit(solution)/shard_map/all_gather | solution.py:31
  95.0 37.2 %copy-start.3 = (u32[32]{0:T(128)S(1)}, u32[32]{0:T(128)}, u32[]{:S(2)}) copy-start(u32[32]{0:T(128)} %constant.20) | copy-start | bytes 388
  95.0 80.9 %all-reduce.3.cloned.1.call-start = ((), (), s32[]{:S(2)}) async-start(), calls=%async_computation.4 | async-start | bytes 327680
Sparse Core Ops, SparseCore 0:
  8.9 35.2 all-gather.3
  72.5 9.0 reduce-scatter.1
  95.1 10.3 all-gather.5
  132.2 43.6 all-reduce.2
where the time goes:
time: 204 us; the launch traced here: 203 us
  waiting for transfers between devices  78.7 us (39%)
  matrix products  53.9 us (26%)
  blocking collectives  48.4 us (24%)
  between operations  13.9 us (7%)
  local copies, waits for them, and re-layouts  5.96 us (3%)
  other arithmetic  2.31 us (1%)
    unnamed x5, waiting for transfers between devices  43.3 us
    dot_general x1, matrix products, body(): jnp.einsum('tpq,qk->tpk', lines_full, masked, precision=highest)  25.5 us
    all_gather x1, waiting for transfers between devices, body(): panel_full = lax.all_gather(panel_factors, 'aux', axis=0, tiled=True)  24.9 us
    dot_general x1, matrix products, body(): polar_line = jnp.einsum('tpk,qk->tpq', scaled, masked, precision=highest)  22.1 us
    psum x1, blocking collectives, body(): return lax.psum(partial_value, 'aux')  20 us
    all_gather x1, blocking collectives, body(): inverse = lax.all_gather(screening, 'aux', axis=1, tiled=True)  18.2 us
    all_gather x1, waiting for transfers between devices, body(): lines_full = lax.all_gather(screened, 'pair', axis=2, tiled=True)  10.5 us
    all_gather x1, blocking collectives, body(): weights_all = lax.all_gather(time_weights, 'tm', axis=0, tiled=True)  10.3 us
  transfers between devices with their start and end apart: 4, of which 3 were waited for; matrix products, arithmetic and copies ran while one was open for 1% of the time, Pallas kernels for 0%

commit v1 on v0

--- a/solution.py
+++ b/solution.py
@@ -15,7 +15,16 @@
 def body(factors, panel_factors, time_weights, tile_mask, forward_table, screening, back_table):
     highest = lax.Precision.HIGHEST
     masked = factors.astype(jnp.float32) * expand_tiles(tile_mask).astype(jnp.float32)
-    panel_full = lax.all_gather(panel_factors, "aux", axis=0, tiled=True)
+    slots = lax.axis_size("aux")
+    formed = sorted(((at, (at + 1) % slots) for at in range(slots)))
+    field_out = panel_factors
+    crops = [field_out]
+    for i in range(1, slots):
+        field_out = lax.ppermute(field_out, axis_name="aux", perm=formed)
+        crops.insert(0, field_out)
+    x_new = jnp.concatenate(crops, 0)
+    piece_next = lax.axis_index("aux") + 1
+    panel_full = jnp.roll(x_new, piece_next * panel_factors.shape[0], axis=0)
     panel_wide = panel_full.astype(jnp.float32)
     freq_count = screening.shape[0]
     first_freq = lax.axis_index("tm") * freq_count

time: 204 us -> 199 us (0.975)
  waiting for transfers between devices: 78.7 us -> 73.2 us
  starting transfers between devices: 0.12 us -> 3.14 us
    all_gather x1 -> x0, waiting for transfers between devices: 24.9 us -> none  [body(): panel_full = lax.all_gather(panel_factors, 'aux', axis=0, tiled=True)]
    ppermute x0 -> x3, waiting for transfers between devices: none -> 20.6 us  [body(): field_out = lax.ppermute(field_out, axis_name='aux', perm=formed)]
    ppermute x0 -> x3, starting transfers between devices: none -> 3.06 us  [body(): field_out = lax.ppermute(field_out, axis_name='aux', perm=formed)]
    unnamed x5 -> x4, waiting for transfers between devices: 43.3 us -> 42.6 us
    unnamed x11 -> x20, local copies, waits for them, and re-layouts: 5.29 us -> 5.46 us
  transfers between devices with their start and end apart: 4 -> 6, of which waited for: 3 -> 4; matrix products, arithmetic and copies ran while one was open for 1% -> 1% of each run, Pallas kernels for 0% -> 0%
where the time goes in v1:
time: 199 us; the launch traced here: 198 us
  waiting for transfers between devices  73.2 us (37%)
  matrix products  54 us (27%)
  blocking collectives  46.9 us (24%)
  between operations  13.9 us (7%)
  local copies, waits for them, and re-layouts  6.15 us (3%)
  starting transfers between devices  3.14 us (2%)
    unnamed x4, waiting for transfers between devices  42.6 us
    dot_general x1, matrix products, body(): jnp.einsum('tpq,qk->tpk', lines_full, masked, precision=highest)  25.5 us
    dot_general x1, matrix products, body(): polar_line = jnp.einsum('tpk,qk->tpq', scaled, masked, precision=highest)  22.2 us
    ppermute x3, waiting for transfers between devices, body(): field_out = lax.ppermute(field_out, axis_name='aux', perm=formed)  20.6 us
    psum x1, blocking collectives, body(): return lax.psum(partial_value, 'aux')  20 us
    all_gather x1, blocking collectives, body(): inverse = lax.all_gather(screening, 'aux', axis=1, tiled=True)  18.3 us
    all_gather x1, waiting for transfers between devices, body(): lines_full = lax.all_gather(screened, 'pair', axis=2, tiled=True)  10 us
    all_gather x1, blocking collectives, body(): weights_all = lax.all_gather(time_weights, 'tm', axis=0, tiled=True)  8.62 us
  transfers between devices with their start and end apart: 6, of which 4 were waited for; matrix products, arithmetic and copies ran while one was open for 1% of the time, Pallas kernels for 0%

profile of v1, /device:TPU:0, one launch (start us, length us, event | category | flops | bytes accessed | tf_op | source)
XLA Modules:
  0.0 198.4 jit_solution(3093512476789765516)
XLA Ops:
  6.5 3.1 %collective-permute-start = (bf16[64,2560]{1,0:T(8,128)(2,1)}, bf16[64,2560]{1,0:T(8,128)(2,1)S(1)}, u32[]{:S(2)}, u32[]{:S(2)}) collective-permute-start(bf16[64,2560]{1,0:T(8,128)(2,1)} %param.8), channel_id=1, source_target_pairs={{0,2},{2,4},{4,6},{6,0},{1,3},{3,5},{5,7},{7,1},{8,10},{10,12},{12... | collective-permute-start | bytes 983048 | tf_op jit(solution)/shard_map/ppermute | solution.py:23
  9.6 10.0 %collective-permute-done = bf16[64,2560]{1,0:T(8,128)(2,1)S(1)} collective-permute-done((bf16[64,2560]{1,0:T(8,128)(2,1)}, bf16[64,2560]{1,0:T(8,128)(2,1)S(1)}, u32[]{:S(2)}, u32[]{:S(2)}) %collective-permute-start) | collective-permute-done | bytes 327712 | tf_op jit(solution)/shard_map/ppermute | solution.py:23
  19.6 0.0 collective-permute-start.1
  19.6 10.7 %collective-permute-done.1 = bf16[64,2560]{1,0:T(8,128)(2,1)S(1)} collective-permute-done((bf16[64,2560]{1,0:T(8,128)(2,1)S(1)}, bf16[64,2560]{1,0:T(8,128)(2,1)S(1)}, u32[]{:S(2)}, u32[]{:S(2)}) %collective-permute-start.1) | collective-permute-done | bytes 327712 | tf_op jit(solution)/shard_map/ppermute | solution.py:23
  30.2 0.0 collective-permute-start.2
  30.2 8.6 %all-gather = f32[4,3,2560]{2,1,0:T(4,128)S(1)} all-gather(f32[1,3,2560]{2,1,0:T(4,128)} %bitcast.22), channel_id=1, replica_groups=mesh['tm'=4,'aux'=4,'pair'=2] {'tm'}, dimensions={0}, use_global_device_ids=true | all-gather | bytes 153600 | tf_op jit(solution)/shard_map/all_gather | solution.py:31
  38.9 0.1 reshape.6
  38.9 0.7 convert_element_type.15
  39.6 0.9 fusion.11
  40.5 0.0 collective-permute-done.2
  40.8 0.3 dynamic-slice_convert_fusion
  41.1 0.0 copy-start.2
  41.1 0.7 broadcast_in_dim.2
  41.8 3.7 %copy-done.1 = f32[6,128,20,128]{3,2,1,0:T(8,128)} copy-done((f32[6,128,20,128]{3,2,1,0:T(8,128)}, f32[6,128,20,128]{3,2,1,0:T(8,128)S(1)}, u32[]{:S(2)}) %copy-start.1) | copy-done | bytes 7864344
  45.5 22.2 %fusion.1 = f32[3,256,768]{2,1,0:T(8,128)} fusion(f32[96,8,20,128]{3,2,1,0:T(8,128)S(1)} %bitcast.20, bf16[768,2560]{1,0:T(8,128)(2,1)S(1)} %copy-done.2, f32[3,2560]{1,0:T(4,128)S(1)} %fusion.11, f32[256,2560]{1,0:T(8,128)S(1)} %dynamic-slice_convert_fusion), kind=kOutput, calls=%fused_computation.3 | convolution fusion | flops 18125291520 | bytes 16807936 | tf_op jit(solution)/shard_map/tpk,qk->tpq/dot_general | solution.py:35
  67.7 0.0 reduce-scatter.2.cloned.1.call-update
  67.7 0.0 all-gather.3.cloned.1.call-start
  67.8 18.3 %all_gather.10 = f32[3,256,256]{2,1,0:T(8,128)S(1)} all-gather(f32[3,64,256]{2,1,0:T(8,128)} %param.12), channel_id=1, replica_groups=mesh['tm'=4,'aux'=4,'pair'=2] {'aux'}, dimensions={1}, use_global_device_ids=true | all-gather | bytes 983040 | tf_op jit(solution)/shard_map/all_gather | solution.py:37
  86.1 4.3 %convolution_bitcast_fusion = f32[3,256,384]{1,2,0:T(8,128)} fusion(f32[3,256,384]{2,1,0:T(8,128)} %reduce-scatter.2.cloned.1.call-done, f32[3,256,256]{2,1,0:T(8,128)S(1)} %all_gather.10), kind=kOutput, calls=%fused_computation.7 | convolution fusion | flops 905969664 | bytes 3145728 | tf_op jit(solution)/shard_map/wpr,wrq->wpq/dot_general | solution.py:38
  90.5 0.0 all-gather.3.cloned.1.call-update
  90.5 0.0 copy-start.4
  90.5 0.0 all-reduce.3.cloned.1.call-start
  90.6 10.0 %all-gather.3.cloned.1.call-done = f32[3,256,768]{1,2,0:T(8,128)} async-done(((f32[3,256,384]{1,2,0:T(8,128)}), f32[3,256,768]{1,2,0:T(8,128)}) %all-gather.3.cloned.1.call-update) | async-done | bytes 2359312 | tf_op jit(solution)/shard_map/all_gather | solution.py:40
  100.6 25.5 %multiply_reduce_fusion = f32[3,2560]{1,0:T(4,128)S(1)} fusion(f32[3,256,768]{1,2,0:T(8,128)} %all-gather.3.cloned.1.call-done, f32[96,8,20,128]{3,2,1,0:T(8,128)} %bitcast.21, bf16[768,2560]{1,0:T(8,128)(2,1)} %param.7, f32[256,2560]{1,0:T(8,128)S(1)} %dynamic-slice_convert_fusion), kind=kOutput, calls=%fused_computation.2 | convolution fusion | flops 18127249408 | bytes 16807936 | tf_op jit(solution)/shard_map/tpq,qk->tpk/dot_general | solution.py:41
  126.1 0.0 copy-done
  126.1 1.0 fusion.7
  127.2 0.0 all-reduce.3.cloned.1.call-update
  127.2 0.0 copy-done.4
  127.2 0.6 dynamic-slice
  128.4 42.5 %all-reduce.3.cloned.1.call-done = f32[12,2560]{1,0:T(8,128)} async-done(((f32[12,2560]{1,0:T(8,128)}), f32[12,2560]{1,0:T(8,128)}) %all-reduce.3.cloned.1.call-update) | async-done | bytes 122896
  171.0 0.9 constant_dynamic-slice_fusion
  171.9 20.0 %psum.7 = f32[3,2560]{1,0:T(4,128)} all-reduce(f32[3,2560]{1,0:T(4,128)S(1)} %constant_dynamic-slice_fusion), channel_id=1, replica_groups=mesh['tm'=4,'aux'=4,'pair'=2] {'aux'}, use_global_device_ids=true, to_apply=%region_3.4 | all-reduce | flops 7680 | bytes 61440 | tf_op jit(solution)/shard_map/psum | solution.py:47
  (15 shorter events, 0.2 us)
Async XLA Ops:
  6.5 119.6 %copy-start = (f32[12,12]{1,0:T(8,128)S(1)}, f32[12,12]{1,0:T(8,128)}, u32[]{:S(2)}) copy-start(f32[12,12]{1,0:T(8,128)} %param.13) | copy-start | bytes 1732
  6.5 34.1 %copy-start.3 = (bf16[64,2560]{1,0:T(8,128)(2,1)S(1)}, bf16[64,2560]{1,0:T(8,128)(2,1)}, u32[]{:S(2)}) copy-start(bf16[64,2560]{1,0:T(8,128)(2,1)} %param.8) | copy-start | bytes 983044
  6.5 79.6 %reduce-scatter.2.cloned.1.call-start = ((), (), s32[]{:S(2)}) async-start(), calls=%async_computation.1 | async-start | bytes 3538944 | tf_op jit(solution)/shard_map/reduce_scatter | solution.py:36
  6.5 13.0 %collective-permute-start = (bf16[64,2560]{1,0:T(8,128)(2,1)}, bf16[64,2560]{1,0:T(8,128)(2,1)S(1)}, u32[]{:S(2)}, u32[]{:S(2)}) collective-permute-start(bf16[64,2560]{1,0:T(8,128)(2,1)} %param.8), channel_id=1, source_target_pairs={{0,2},{2,4},{4,6},{6,0},{1,3},{3,5},{5,7},{7,1},{8,10},{10,12},{12... | collective-permute-start | bytes 983048 | tf_op jit(solution)/shard_map/ppermute | solution.py:23
  19.6 10.7 %collective-permute-start.1 = (bf16[64,2560]{1,0:T(8,128)(2,1)S(1)}, bf16[64,2560]{1,0:T(8,128)(2,1)S(1)}, u32[]{:S(2)}, u32[]{:S(2)}) collective-permute-start(bf16[64,2560]{1,0:T(8,128)(2,1)S(1)} %collective-permute-done), channel_id=1, source_target_pairs={{0,2},{2,4},{4,6},{6,0},{1,3},{3,5},{5,7},{7,1},{8,10},{10,12},{12... | collective-permute-start | bytes 983048 | tf_op jit(solution)/shard_map/ppermute | solution.py:23
  30.2 10.3 %collective-permute-start.2 = (bf16[64,2560]{1,0:T(8,128)(2,1)S(1)}, bf16[64,2560]{1,0:T(8,128)(2,1)S(1)}, u32[]{:S(2)}, u32[]{:S(2)}) collective-permute-start(bf16[64,2560]{1,0:T(8,128)(2,1)S(1)} %collective-permute-done.1), channel_id=1, source_target_pairs={{0,2},{2,4},{4,6},{6,0},{1,3},{3,5},{5,7},{7,1},{8,10},{10,12},{12... | collective-permute-start | bytes 983048 | tf_op jit(solution)/shard_map/ppermute | solution.py:23
  41.1 4.4 %copy-start.2 = (bf16[768,2560]{1,0:T(8,128)(2,1)S(1)}, bf16[768,2560]{1,0:T(8,128)(2,1)}, u32[]{:S(2)}) copy-start(bf16[768,2560]{1,0:T(8,128)(2,1)} %param.7) | copy-start | bytes 11796484
  41.8 3.7 %copy-start.1 = (f32[6,128,20,128]{3,2,1,0:T(8,128)}, f32[6,128,20,128]{3,2,1,0:T(8,128)S(1)}, u32[]{:S(2)}) copy-start(f32[6,128,20,128]{3,2,1,0:T(8,128)S(1)} %broadcast_in_dim.2) | copy-start | bytes 23592964
  67.7 32.8 %all-gather.3.cloned.1.call-start = ((), (), s32[]{:S(2)}) async-start(), calls=%async_computation.2 | async-start | bytes 3538944 | tf_op jit(solution)/shard_map/all_gather | solution.py:40
  90.5 36.7 %copy-start.4 = (u32[32]{0:T(128)S(1)}, u32[32]{0:T(128)}, u32[]{:S(2)}) copy-start(u32[32]{0:T(128)} %constant.49) | copy-start | bytes 388
  90.5 80.4 %all-reduce.3.cloned.1.call-start = ((), (), s32[]{:S(2)}) async-start(), calls=%async_computation.3 | async-start | bytes 327680
Sparse Core Ops, SparseCore 0:
  67.9 10.4 reduce-scatter.1
  90.6 9.9 all-gather.2
  127.3 43.6 all-reduce.2
